TPU v7x, 512 devices: a whole 4x4x16 slice. The times are simulated.
512 devices in a mesh: space: 16 (over z_hi, x), inst: 32 (over y, z_lo, core).
Axes of the slice: x: 4, y: 4, z: 16 (z_hi: 4, z_lo: 4; z = z_hi * 4 + z_lo), core: 2. Of those that a mesh axis runs over, the one named last changes fastest.
Arguments:
- flow_state: float32 [32, 7, 65536], P('inst', None, 'space'), may hold values from -5.5 to 5.5
- face_nbr: int32 [6, 65536], P(None, 'space'), may hold values from 0 to 5119
- halo_send: int32 [2, 8192], P(None, 'space'), may hold values from 0 to 4095, as said below
- face_area: float32 [3, 6, 65536], P(None, None, 'space'), may hold values from -3 to 3
- cell_volume: float32 [65536], P(('space', 'inst')), may hold values from 0.5 to 2
- flux_left: float32 [7, 7], replicated, may hold values from -2 to 2
- flux_right: float32 [7, 7], replicated, may hold values from -2 to 2
Outputs:
- inverse: float32 [2, 7, 7, 16, 65536], P(None, None, None, None, ('space', 'inst'))
Inputs may be any that keep to these rules, and one draw needn't show every extreme that they name: `halo_send`: within each slab's block of 512 columns, row 0 lists each cell of local indices (7) * 512 to 4095 once and row 1 each cell of local indices 0 to 511 once.
All inputs are finite; a program needn't handle non-finite values.
Results may differ from a plain program's by a relative error of at most 0.0001.
Values sent between devices are 32-bit elements; how exact they have to be, the bound alone decides.
A program may use at most 128 MiB of HBM per device.

v0:
```python
import jax
import jax.numpy as jnp
from jax import lax
from jax.sharding import PartitionSpec as P

INSTANCES = 32
HARM = 16
frequency = 0.1


def shifted(block, axis, distance):
    devices = range(lax.axis_size(axis))
    route = [(i - distance, i) for i in devices if i - distance in devices]
    return lax.ppermute(block, axis, route)


def face_jacobian(face_mean, normal_flux, flux_left, flux_right):
    coupling = flux_left[:, :, None] * flux_right[None, :, :]
    jacobian = jnp.einsum("imj,bmc->bijc", coupling, face_mean, precision=lax.Precision.HIGHEST)
    identity = jnp.eye(face_mean.shape[1], dtype=jnp.float32)
    jacobian = jacobian + normal_flux[:, None, None, :] * identity[None, :, :, None]
    spectral = jnp.max(jnp.sum(jnp.abs(jacobian), axis=2), axis=1) + 0.5
    return (jacobian, spectral, identity)


def face_terms(face_mean, normal_flux, flux_left, flux_right):
    jacobian, spectral, identity = face_jacobian(face_mean, normal_flux, flux_left, flux_right)
    return jnp.sum(
        0.5 * (jacobian + spectral[:, None, None, :] * identity[None, :, :, None]), axis=0
    )


def invert(real_part, imag_part):
    size_vars = real_part.shape[0]
    identity = jnp.broadcast_to(
        jnp.eye(size_vars, dtype=jnp.float32)[:, :, None, None], real_part.shape
    )
    aug_real = jnp.concatenate([real_part, identity], axis=1)
    aug_imag = jnp.concatenate([imag_part, jnp.zeros_like(identity)], axis=1)
    for column in range(size_vars):
        lead_real = aug_real[column, column]
        lead_imag = aug_imag[column, column]
        inverse_norm = 1.0 / (lead_real * lead_real + lead_imag * lead_imag)
        recip_real = lead_real * inverse_norm
        recip_imag = -lead_imag * inverse_norm
        row_real = aug_real[column] * recip_real - aug_imag[column] * recip_imag
        row_imag = aug_real[column] * recip_imag + aug_imag[column] * recip_real
        col_real = aug_real[:, column : column + 1]
        col_imag = aug_imag[:, column : column + 1]
        aug_real = aug_real - (col_real * row_real[None] - col_imag * row_imag[None])
        aug_imag = aug_imag - (col_real * row_imag[None] + col_imag * row_real[None])
        aug_real = aug_real.at[column].set(row_real)
        aug_imag = aug_imag.at[column].set(row_imag)
    return (aug_real[:, size_vars:], aug_imag[:, size_vars:])


def per_device(flow_state, face_nbr, halo_send, face_area, cell_volume, flux_left, flux_right):
    components = flow_state.shape[1]
    cell_count = flow_state.shape[2]
    face_count = face_nbr.shape[0]
    owners = lax.axis_size("inst")
    share_cells = cell_count // owners
    upward = flow_state[:, :, halo_send[0]]
    downward = flow_state[:, :, halo_send[1]]
    from_lower = shifted(upward, "space", 1)
    from_upper = shifted(downward, "space", -1)
    extended = jnp.concatenate([flow_state, from_lower, from_upper], axis=2)
    running = jnp.zeros((components, components, cell_count), jnp.float32)
    for direction in range(face_count):
        neighbour = jnp.take(extended, face_nbr[direction], axis=2)
        face_mean = 0.5 * (flow_state + neighbour)
        normals = face_area[:, direction]
        normal_flux = (
            face_mean[:, 1] * normals[0]
            + face_mean[:, 2] * normals[1]
            + face_mean[:, 3] * normals[2]
        )
        face_mean, normal_flux = (face_mean, normal_flux)
        running = running + face_terms(face_mean, normal_flux, flux_left, flux_right)
    everything = lax.psum(running, "inst")
    summed = lax.dynamic_slice_in_dim(
        everything, lax.axis_index("inst") * share_cells, share_cells, 2
    )
    jacobian_mean = summed / (face_count * INSTANCES)
    harmonics = jnp.arange(1, HARM + 1, dtype=jnp.int32).astype(jnp.float32)
    imag_shift = harmonics[:, None] * frequency * cell_volume[None, :]
    real_part = jnp.broadcast_to(
        jacobian_mean[:, :, None, :], (components, components, HARM, share_cells)
    )
    imag_part = jnp.eye(components, dtype=jnp.float32)[:, :, None, None] * imag_shift[None, None]
    inv_real, inv_imag = invert(real_part, imag_part)
    return jnp.stack([inv_real, inv_imag])


def solution(mesh):
    placed = (
        P("inst", None, "space"),
        P(None, "space"),
        P(None, "space"),
        P(None, None, "space"),
        P(("space", "inst")),
        P(),
        P(),
    )
    return jax.shard_map(
        per_device,
        mesh=mesh,
        in_specs=placed,
        out_specs=P(None, None, None, None, ("space", "inst")),
        check_vma=False,
    )
```

profile of v0, /device:TPU:2, one launch (start us, length us, event | category | flops | bytes accessed | tf_op | source)
XLA Modules:
  0.0 463.7 jit_solution(6853187282242230879)
XLA Ops:
  6.5 0.0 all-reduce.3.cloned.1.call-start
  6.5 1.6 copy.196
  8.1 0.0 copy-done.11
  8.1 0.0 copy-start
  8.2 1.0 gather_fusion
  9.2 3.4 collective-permute-start
  12.7 1.0 gather_fusion.1
  13.7 5.7 %collective-permute-start.1 = (f32[1,7,512]{1,2,0:T(8,128)S(1)}, f32[1,7,512]{1,2,0:T(8,128)S(1)}, u32[]{:S(2)}, u32[]{:S(2)}) collective-permute-start(f32[1,7,512]{1,2,0:T(8,128)S(1)} %bitcast.361), channel_id=1, source_target_pairs={{32,0},{64,32},{96,64},{128,96},{160,128},{192,160},{224,192},{256... | collective-permute-start | bytes 43016 | tf_op jit(solution)/shard_map/ppermute | solution.py:14
  19.4 0.0 copy-done.5
  19.4 0.1 fusion.97
  19.5 0.6 compare_and_fusion
  20.2 0.6 compare_and_fusion.2
  20.8 0.6 compare_and_fusion.4
  21.4 0.0 copy-done.12
  21.4 0.1 copy.199
  21.5 0.0 collective-permute-done
  21.5 0.0 copy-done
  21.5 1.9 collective-permute-done.1
  23.4 1.8 maximum_bitcast_fusion
  25.1 14.2 %gather_fusion.2 = f32[4096,7]{1,0:T(8,128)} fusion(f32[7,5120]{0,1:T(8,128)S(1)} %maximum_bitcast_fusion, s32[4096]{0:T(1024)S(1)} %fusion.74), kind=kCustom, calls=%fused_computation.clone | custom fusion | bytes 245760 | tf_op jit(solution)/shard_map/jit(_take)/gather | solution.py:70
  39.3 2.2 copy.197
  41.5 14.2 %gather_fusion.3 = f32[4096,7]{1,0:T(8,128)} fusion(f32[7,5120]{0,1:T(8,128)S(1)} %maximum_bitcast_fusion, s32[4096]{0:T(1024)S(1)} %fusion.75), kind=kCustom, calls=%fused_computation.1.clone | custom fusion | bytes 245760 | tf_op jit(solution)/shard_map/jit(_take)/gather | solution.py:70
  55.7 2.2 copy.200
  57.9 14.2 %gather_fusion.4 = f32[4096,7]{1,0:T(8,128)} fusion(f32[7,5120]{0,1:T(8,128)S(1)} %maximum_bitcast_fusion, s32[4096]{0:T(1024)S(1)} %fusion.76), kind=kCustom, calls=%fused_computation.2.clone | custom fusion | bytes 245760 | tf_op jit(solution)/shard_map/jit(_take)/gather | solution.py:70
  72.1 2.2 copy.202
  74.3 14.2 %gather_fusion.5 = f32[4096,7]{1,0:T(8,128)} fusion(f32[7,5120]{0,1:T(8,128)S(1)} %maximum_bitcast_fusion, s32[4096]{0:T(1024)S(1)} %fusion.77), kind=kCustom, calls=%fused_computation.3.clone | custom fusion | bytes 245760 | tf_op jit(solution)/shard_map/jit(_take)/gather | solution.py:70
  88.5 2.9 copy.204
  91.3 14.2 %gather_fusion.6 = f32[4096,7]{1,0:T(8,128)} fusion(f32[7,5120]{0,1:T(8,128)S(1)} %maximum_bitcast_fusion, s32[4096]{0:T(1024)S(1)} %fusion.78), kind=kCustom, calls=%fused_computation.4.clone | custom fusion | bytes 245760 | tf_op jit(solution)/shard_map/jit(_take)/gather | solution.py:70
  105.5 2.9 copy.206
  108.4 14.2 %gather_fusion.7 = f32[4096,7]{1,0:T(8,128)} fusion(f32[7,5120]{0,1:T(8,128)S(1)} %maximum_bitcast_fusion, s32[4096]{0:T(1024)S(1)} %fusion.79), kind=kCustom, calls=%fused_computation.5.clone | custom fusion | bytes 245760 | tf_op jit(solution)/shard_map/jit(_take)/gather | solution.py:70
  122.5 0.0 copy-start.6
  122.5 0.0 copy-start.7
  122.6 0.0 copy-start.8
  122.6 0.0 copy-start.9
  122.6 0.0 copy-start.10
  122.6 0.0 copy-start.4
  122.6 2.3 copy.208
  124.9 0.0 copy-done.3
  125.0 0.2 fusion.7
  125.2 1.6 fusion.36
  126.8 0.0 copy-done.4
  126.8 1.1 abs_reduce_fusion.5
  128.0 1.1 abs_reduce_fusion.4
  129.2 1.1 abs_reduce_fusion.3
  130.4 1.6 fusion.30
  132.1 2.1 abs_reduce_fusion.2
  134.2 2.1 abs_reduce_fusion.1
  136.3 2.1 abs_reduce_fusion
  138.5 0.0 copy-start.13
  138.5 3.3 multiply_bitcast_fusion
  141.8 0.0 all-reduce.3.cloned.1.call-update
  141.8 0.1 broadcast_multiply_fusion.1
  141.9 0.1 broadcast_multiply_fusion
  142.0 310.4 %all-reduce.3.cloned.1.call-done = f32[7,7,4096]{2,1,0:T(8,128)} async-done(((f32[7,7,4096]{2,1,0:T(8,128)}), f32[7,7,4096]{2,1,0:T(8,128)}) %all-reduce.3.cloned.1.call-update) | async-done | bytes 802832 | tf_op jit(solution)/shard_map/psum | solution.py:80
  452.5 0.8 dynamic-slice_multiply_fusion
  453.3 0.1 broadcast_in_dim.22
  453.5 0.2 fusion.6
  453.8 0.2 subtract_subtract_fusion.5
  454.2 0.2 subtract_subtract_fusion.4
  454.5 0.2 subtract_subtract_fusion.3
  454.9 0.2 subtract_subtract_fusion.2
  455.2 0.2 subtract_subtract_fusion.1
  455.6 0.2 subtract_subtract_fusion
  455.9 1.0 pad_maximum_fusion.1
  (78 shorter events, 1.0 us)
Async XLA Ops:
  6.5 1.6 copy-start.11
  6.5 12.9 %copy-start.5 = (s32[6,4096]{1,0:T(8,128)S(1)}, s32[6,4096]{1,0:T(8,128)}, u32[]{:S(2)}) copy-start(s32[6,4096]{1,0:T(8,128)} %param.38) | copy-start | bytes 294916
  6.5 14.9 %copy-start.12 = (f32[7,7]{1,0:T(8,128)S(1)}, f32[7,7]{1,0:T(8,128)}, u32[]{:S(2)}) copy-start(f32[7,7]{1,0:T(8,128)} %param.43) | copy-start | bytes 592
  6.5 445.9 %all-reduce.3.cloned.1.call-start = ((), (), s32[]{:S(2)}) async-start(), calls=%async_computation | async-start | bytes 1835008 | tf_op jit(solution)/shard_map/psum | solution.py:80
  8.1 13.4 %copy-start = (f32[1,7,4096]{1,2,0:T(8,128)}, f32[1,7,4096]{1,2,0:T(8,128)S(1)}, u32[]{:S(2)}) copy-start(f32[1,7,4096]{1,2,0:T(8,128)S(1)} %copy.196) | copy-start | bytes 344068
  9.2 12.3 %collective-permute-start = (f32[1,7,512]{1,2,0:T(8,128)S(1)}, f32[1,7,512]{1,2,0:T(8,128)S(1)}, u32[]{:S(2)}, u32[]{:S(2)}) collective-permute-start(f32[1,7,512]{1,2,0:T(8,128)S(1)} %bitcast.360), channel_id=1, source_target_pairs={{0,32},{32,64},{64,96},{96,128},{128,160},{160,192},{192,224},{224... | collective-permute-start | bytes 43016 | tf_op jit(solution)/shard_map/ppermute | solution.py:14
  13.7 9.7 %collective-permute-start.1 = (f32[1,7,512]{1,2,0:T(8,128)S(1)}, f32[1,7,512]{1,2,0:T(8,128)S(1)}, u32[]{:S(2)}, u32[]{:S(2)}) collective-permute-start(f32[1,7,512]{1,2,0:T(8,128)S(1)} %bitcast.361), channel_id=1, source_target_pairs={{32,0},{64,32},{96,64},{128,96},{160,128},{192,160},{224,192},{256... | collective-permute-start | bytes 43016 | tf_op jit(solution)/shard_map/ppermute | solution.py:14
  122.5 2.4 copy-start.1
  122.5 2.4 copy-start.2
  122.5 2.4 copy-start.3
  122.5 2.4 copy-start.6
  122.5 2.4 copy-start.7
  122.6 2.4 copy-start.8
  122.6 2.4 copy-start.9
  122.6 2.4 copy-start.10
  122.6 4.2 copy-start.4
  138.5 3.3 copy-start.13
Sparse Core Ops, SparseCore 0:
  141.9 310.5 all-reduce.2
where the time goes:
time: 464 us
  waiting for transfers between devices  312 us (67%)
  local copies, waits for them, and re-layouts  104 us (22%)
  other arithmetic  14.7 us (3%)
  between operations  14.1 us (3%)
  matrix products  9.63 us (2%)
  starting transfers between devices  9.13 us (2%)
    psum x1, waiting for transfers between devices, per_device(): everything = lax.psum(running, 'inst')  310 us
    gather x12, local copies, waits for them, and re-layouts, per_device(): neighbour = jnp.take(extended, face_nbr[direction], axis=2)  99.7 us
    dot_general x6, matrix products, face_jacobian(): jnp.einsum('imj,bmc->bijc', coupling, face_mean, precision=lax.Precision....  9.63 us
  transfers between devices with their start and end apart: 3, of which 2 were waited for; matrix products, arithmetic and copies ran while one was open for 1% of the time, Pallas kernels for 0%

commit v1 on v0

--- a/solution.py
+++ b/solution.py
@@ -77,7 +77,7 @@
         )
         face_mean, normal_flux = (face_mean, normal_flux)
         running = running + face_terms(face_mean, normal_flux, flux_left, flux_right)
-    everything = lax.psum(running, "inst")
+    everything = jnp.sum(lax.all_gather(running, "inst"), axis=0)
     summed = lax.dynamic_slice_in_dim(
         everything, lax.axis_index("inst") * share_cells, share_cells, 2
     )

time: 464 us -> 361 us (0.78)
  the two profiles are of different devices: /device:TPU:2 before, /device:TPU:1 now
where the time goes in v1:
time: 361 us
  waiting for transfers between devices  203 us (56%)
  local copies, waits for them, and re-layouts  104 us (29%)
  other arithmetic  25.1 us (7%)
  between operations  14.1 us (4%)
  matrix products  9.65 us (3%)
  starting transfers between devices  5.26 us (1%)
    all_gather x1, waiting for transfers between devices, per_device(): everything = jnp.sum(lax.all_gather(running, 'inst'), axis=0)  199 us
    gather x12, local copies, waits for them, and re-layouts, per_device(): neighbour = jnp.take(extended, face_nbr[direction], axis=2)  99.7 us
    reduce_sum x1, other arithmetic, per_device(): everything = jnp.sum(lax.all_gather(running, 'inst'), axis=0)  10.9 us
    dot_general x6, matrix products, face_jacobian(): jnp.einsum('imj,bmc->bijc', coupling, face_mean, precision=lax.Precision....  9.65 us
  transfers between devices with their start and end apart: 3, of which 2 were waited for; matrix products, arithmetic and copies ran while one was open for 1% of the time, Pallas kernels for 0%

profile of v1, /device:TPU:1, one launch (start us, length us, event | category | flops | bytes accessed | tf_op | source)
XLA Modules:
  0.0 361.0 jit_solution(4329143518022592939)
XLA Ops:
  6.5 0.0 all-gather.2.cloned.1.call-start
  6.5 1.6 copy.196
  8.1 0.0 copy-done.11
  8.1 0.0 copy-start
  8.2 1.0 gather_fusion
  9.2 4.0 %collective-permute-start = (f32[1,7,512]{1,2,0:T(8,128)S(1)}, f32[1,7,512]{1,2,0:T(8,128)S(1)}, u32[]{:S(2)}, u32[]{:S(2)}) collective-permute-start(f32[1,7,512]{1,2,0:T(8,128)S(1)} %bitcast.358), channel_id=1, source_target_pairs={{0,32},{32,64},{64,96},{96,128},{128,160},{160,192},{192,224},{224... | collective-permute-start | bytes 43016 | tf_op jit(solution)/shard_map/ppermute | solution.py:14
  13.2 1.0 gather_fusion.1
  14.3 1.3 collective-permute-start.1
  15.6 0.0 copy-done.5
  15.6 0.1 fusion.97
  15.7 0.6 compare_and_fusion
  16.3 0.6 compare_and_fusion.2
  16.9 0.6 compare_and_fusion.4
  17.5 0.0 copy-done.12
  17.5 0.1 copy.199
  17.6 0.0 collective-permute-done
  17.6 0.0 copy-done
  17.6 3.7 %collective-permute-done.1 = f32[1,7,512]{1,2,0:T(8,128)S(1)} collective-permute-done((f32[1,7,512]{1,2,0:T(8,128)S(1)}, f32[1,7,512]{1,2,0:T(8,128)S(1)}, u32[]{:S(2)}, u32[]{:S(2)}) %collective-permute-start.1) | collective-permute-done | bytes 14368 | tf_op jit(solution)/shard_map/ppermute | solution.py:14
  21.4 1.8 maximum_bitcast_fusion
  23.1 14.2 %gather_fusion.2 = f32[4096,7]{1,0:T(8,128)} fusion(f32[7,5120]{0,1:T(8,128)S(1)} %maximum_bitcast_fusion, s32[4096]{0:T(1024)S(1)} %fusion.74), kind=kCustom, calls=%fused_computation.clone | custom fusion | bytes 245760 | tf_op jit(solution)/shard_map/jit(_take)/gather | solution.py:70
  37.3 2.2 copy.197
  39.5 14.2 %gather_fusion.3 = f32[4096,7]{1,0:T(8,128)} fusion(f32[7,5120]{0,1:T(8,128)S(1)} %maximum_bitcast_fusion, s32[4096]{0:T(1024)S(1)} %fusion.75), kind=kCustom, calls=%fused_computation.1.clone | custom fusion | bytes 245760 | tf_op jit(solution)/shard_map/jit(_take)/gather | solution.py:70
  53.7 2.2 copy.200
  55.9 14.2 %gather_fusion.4 = f32[4096,7]{1,0:T(8,128)} fusion(f32[7,5120]{0,1:T(8,128)S(1)} %maximum_bitcast_fusion, s32[4096]{0:T(1024)S(1)} %fusion.76), kind=kCustom, calls=%fused_computation.2.clone | custom fusion | bytes 245760 | tf_op jit(solution)/shard_map/jit(_take)/gather | solution.py:70
  70.1 2.2 copy.202
  72.3 14.2 %gather_fusion.5 = f32[4096,7]{1,0:T(8,128)} fusion(f32[7,5120]{0,1:T(8,128)S(1)} %maximum_bitcast_fusion, s32[4096]{0:T(1024)S(1)} %fusion.77), kind=kCustom, calls=%fused_computation.3.clone | custom fusion | bytes 245760 | tf_op jit(solution)/shard_map/jit(_take)/gather | solution.py:70
  86.5 2.9 copy.204
  89.3 14.2 %gather_fusion.6 = f32[4096,7]{1,0:T(8,128)} fusion(f32[7,5120]{0,1:T(8,128)S(1)} %maximum_bitcast_fusion, s32[4096]{0:T(1024)S(1)} %fusion.78), kind=kCustom, calls=%fused_computation.4.clone | custom fusion | bytes 245760 | tf_op jit(solution)/shard_map/jit(_take)/gather | solution.py:70
  103.5 2.9 copy.206
  106.4 14.2 %gather_fusion.7 = f32[4096,7]{1,0:T(8,128)} fusion(f32[7,5120]{0,1:T(8,128)S(1)} %maximum_bitcast_fusion, s32[4096]{0:T(1024)S(1)} %fusion.79), kind=kCustom, calls=%fused_computation.5.clone | custom fusion | bytes 245760 | tf_op jit(solution)/shard_map/jit(_take)/gather | solution.py:70
  120.6 0.0 copy-start.7
  120.6 0.0 copy-start.8
  120.6 0.0 copy-start.9
  120.6 0.0 copy-start.10
  120.6 0.0 copy-start.4
  120.6 2.3 copy.208
  122.9 0.0 copy-done.1
  122.9 0.0 copy-done.3
  123.0 0.2 fusion.7
  123.2 1.7 fusion.36
  124.9 1.1 abs_reduce_fusion.5
  126.1 1.1 abs_reduce_fusion.4
  127.3 1.1 abs_reduce_fusion.3
  128.5 1.7 fusion.30
  130.2 2.1 abs_reduce_fusion.2
  132.3 2.1 abs_reduce_fusion.1
  134.5 2.1 abs_reduce_fusion
  136.6 0.0 copy-start.13
  136.6 3.4 add_multiply_fusion
  140.0 0.0 all-gather.2.cloned.1.call-update
  140.0 0.0 copy-done.13
  140.0 0.1 broadcast_multiply_fusion.1
  140.1 0.1 broadcast_multiply_fusion
  140.2 199.2 %all-gather.2.cloned.1.call-done = f32[32,7,7,4096]{3,2,1,0:T(8,128)} async-done(((f32[1,7,7,4096]{3,2,1,0:T(8,128)}), f32[32,7,7,4096]{3,2,1,0:T(8,128)}) %all-gather.2.cloned.1.call-update) | async-done | bytes 25690128 | tf_op jit(solution)/shard_map/all_gather | solution.py:80
  339.5 10.9 %reduce_sum.71 = f32[7,7,4096]{2,1,0:T(8,128)S(1)} reduce(f32[32,7,7,4096]{3,2,1,0:T(8,128)} %all-gather.2.cloned.1.call-done, f32[]{:T(128)} %constant.360.clone.1), dimensions={0}, to_apply=%region_12.14 | reduce | flops 6221824 | bytes 26492932 | tf_op jit(solution)/shard_map/reduce_sum | solution.py:80
  350.5 0.1 broadcast_in_dim.22
  350.7 0.2 fusion.6
  351.0 0.2 subtract_subtract_fusion.5
  351.4 0.2 subtract_subtract_fusion.4
  351.7 0.2 subtract_subtract_fusion.3
  352.1 0.2 subtract_subtract_fusion.2
  352.4 0.2 subtract_subtract_fusion.1
  352.8 0.2 subtract_subtract_fusion
  353.1 1.0 pad_maximum_fusion.1
  (79 shorter events, 1.0 us)
Async XLA Ops:
  6.5 1.6 copy-start.11
  6.5 9.0 %copy-start.5 = (s32[6,4096]{1,0:T(8,128)S(1)}, s32[6,4096]{1,0:T(8,128)}, u32[]{:S(2)}) copy-start(s32[6,4096]{1,0:T(8,128)} %param.38) | copy-start | bytes 294916
  6.5 11.0 %copy-start.12 = (f32[7,7]{1,0:T(8,128)S(1)}, f32[7,7]{1,0:T(8,128)}, u32[]{:S(2)}) copy-start(f32[7,7]{1,0:T(8,128)} %param.43) | copy-start | bytes 592
  6.5 332.9 %all-gather.2.cloned.1.call-start = ((), (), s32[]{:S(2)}) async-start(), calls=%async_computation | async-start | bytes 30277632 | tf_op jit(solution)/shard_map/all_gather | solution.py:80
  8.1 9.5 %copy-start = (f32[1,7,4096]{1,2,0:T(8,128)}, f32[1,7,4096]{1,2,0:T(8,128)S(1)}, u32[]{:S(2)}) copy-start(f32[1,7,4096]{1,2,0:T(8,128)S(1)} %copy.196) | copy-start | bytes 344068
  9.2 8.4 %collective-permute-start = (f32[1,7,512]{1,2,0:T(8,128)S(1)}, f32[1,7,512]{1,2,0:T(8,128)S(1)}, u32[]{:S(2)}, u32[]{:S(2)}) collective-permute-start(f32[1,7,512]{1,2,0:T(8,128)S(1)} %bitcast.358), channel_id=1, source_target_pairs={{0,32},{32,64},{64,96},{96,128},{128,160},{160,192},{192,224},{224... | collective-permute-start | bytes 43016 | tf_op jit(solution)/shard_map/ppermute | solution.py:14
  14.3 7.1 %collective-permute-start.1 = (f32[1,7,512]{1,2,0:T(8,128)S(1)}, f32[1,7,512]{1,2,0:T(8,128)S(1)}, u32[]{:S(2)}, u32[]{:S(2)}) collective-permute-start(f32[1,7,512]{1,2,0:T(8,128)S(1)} %bitcast.359), channel_id=1, source_target_pairs={{32,0},{64,32},{96,64},{128,96},{160,128},{192,160},{224,192},{256... | collective-permute-start | bytes 43016 | tf_op jit(solution)/shard_map/ppermute | solution.py:14
  120.5 2.4 copy-start.1
  120.5 2.4 copy-start.2
  120.5 2.4 copy-start.3
  120.5 2.4 copy-start.6
  120.6 2.4 copy-start.7
  120.6 2.4 copy-start.8
  120.6 2.4 copy-start.9
  120.6 2.4 copy-start.10
  120.6 4.3 %copy-start.4 = (f32[7,7]{1,0:T(8,128)S(1)}, f32[7,7]{1,0:T(8,128)}, u32[]{:S(2)}) copy-start(f32[7,7]{1,0:T(8,128)} %param.42) | copy-start | bytes 592
  136.6 3.4 copy-start.13
Sparse Core Ops, SparseCore 0:
  140.1 199.3 all-gather.1
